TPU v7x, 256 devices: a whole 4x4x8 slice. The times are simulated.
256 devices in a mesh: section: 8 (over x, core), dp: 32 (over y, z).
Axes of the slice: x: 4, y: 4, z: 8, core: 2. Of those that a mesh axis runs over, the one named last changes fastest.
Arguments:
- section_inputs: bfloat16 [8, 8, 1024, 8192], P('section', None, 'dp'), may hold values from -6 to 6
- adapter_down: bfloat16 [8, 8192, 128], P('section'), may hold values from -0.0625 to 0.0625
- adapter_up: bfloat16 [8, 8192, 128], P('section'), may hold values from -0.5 to 0.5
- representation: bfloat16 [8, 1024, 8192], P('section', 'dp'), may hold values from -6 to 6
- head_weights: bfloat16 [8192, 128], P('dp'), may hold values from -1 to 1
- head_targets: bfloat16 [8, 1024, 128], P('section', 'dp'), may hold values from -40 to 40
- head_task: int32 [8, 1], replicated, may hold values from 0 to 5
Outputs:
- down_grads: float32 [8, 8192, 128], P('section', 'dp')
- up_grads: float32 [8, 8192, 128], P('section', 'dp')
- task_weights: float32 [6], replicated
Inputs may be any that keep to these rules, and one draw needn't show every extreme that they name: `head_task`: each head belongs to one task, and every task has at least one head.
All inputs are finite; a program needn't handle non-finite values.
Results may differ from a plain program's by a relative error of at most 0.022.
Values may be sent and summed in bfloat16 or wider, within the bound.
No kernel may reach another device: no remote copies, remote signals or barrier semaphores. Data moves between devices by JAX's collectives and lax.ppermute only.
A program may use at most 64 MiB of HBM per device.

v0:
```python
import jax
import jax.numpy as jnp
from jax import lax
from jax.sharding import PartitionSpec as P

HEAD_OUT = 16
TASKS = 6
STEPS = 20
STEP_RATE = 3.0


def from_behind(value, axis, steps):
    count = lax.axis_size(axis)
    first, last = (max(0, -steps), min(count, count - steps))
    return lax.ppermute(value, axis, [(source, source + steps) for source in range(first, last)])


def swish_slope(preact):
    logistic = jax.nn.sigmoid(preact)
    return logistic * (1.0 + preact * (1.0 - logistic))


def section_back(inputs, down_map, up_map, cotangent):
    preact = jnp.dot(inputs, down_map, preferred_element_type=jnp.float32)
    active = jax.nn.silu(preact).astype(jnp.bfloat16)
    branch = jnp.dot(cotangent, up_map, preferred_element_type=jnp.float32)
    inner = (branch * swish_slope(preact)).astype(jnp.bfloat16)
    back = lax.dot_general(
        inner, down_map, (((1,), (1,)), ((), ())), preferred_element_type=jnp.float32
    )
    passed = (cotangent.astype(jnp.float32) + back).astype(jnp.bfloat16)
    return (active, inner, passed)


def store_row(buffer, value, index, valid):
    previous = lax.dynamic_index_in_dim(buffer, index, 0, keepdims=False)
    chosen = jnp.where(valid, value, previous)
    return lax.dynamic_update_index_in_dim(buffer, chosen, index, 0)


def descend(gram_matrix):
    trace_sum = jnp.trace(gram_matrix) + 1e-06
    start = jnp.full((TASKS,), 1.0 / TASKS, dtype=jnp.float32)

    def advance(counter, weights):
        descent = jnp.dot(gram_matrix, weights, precision=lax.Precision.HIGHEST) / trace_sum
        weights = weights * jnp.exp(-STEP_RATE * descent)
        return weights / jnp.sum(weights)

    return lax.fori_loop(0, STEPS, advance, start)


def body(
    section_inputs, adapter_down, adapter_up, representation, head_weights, head_targets, head_task
):
    sections = lax.axis_size("section")
    my_section = lax.axis_index("section")
    micro_count = section_inputs.shape[1]
    tok_rows = section_inputs.shape[2]
    dim_model = section_inputs.shape[3]
    rank_width = adapter_down.shape[2]
    saved = section_inputs[0]
    down_map = adapter_down[0]
    up_map = adapter_up[0]
    weights = lax.all_gather(head_weights, "dp", axis=0, tiled=True)
    predicted = jnp.dot(representation[0], weights, preferred_element_type=jnp.float32)
    residual = (predicted - head_targets[0].astype(jnp.float32)).astype(jnp.bfloat16)
    column_task = jnp.repeat(head_task[:, 0], HEAD_OUT)
    onehot = (column_task[None, :] == jnp.arange(TASKS, dtype=jnp.int32)[:, None]).astype(
        jnp.float32
    )
    masked = residual[None, :, :] * onehot.astype(jnp.bfloat16)[:, None, :]
    task_grads = jnp.einsum("atc,dc->atd", masked, weights, preferred_element_type=jnp.float32)
    partial_gram = jnp.einsum(
        "atd,btd->ab", task_grads, task_grads, precision=lax.Precision.HIGHEST
    )
    gram_matrix = lax.psum(partial_gram, ("section", "dp"))
    mixing = descend(gram_matrix)
    column_weight = jnp.dot(mixing, onehot, precision=lax.Precision.HIGHEST)
    weighted = (residual.astype(jnp.float32) * column_weight[None, :]).astype(jnp.bfloat16)
    own_grad = jnp.einsum(
        "tc,dc->td", weighted, weights, preferred_element_type=jnp.float32
    ).astype(jnp.bfloat16)
    cotangents = lax.all_gather(own_grad[None], "section", axis=0, tiled=True)

    def tick(counter, carry):
        incoming, grad_rows, active_rows, inner_rows = carry
        micro_index = counter - (sections - 1 - my_section)
        valid = (micro_index >= 0) & (micro_index < micro_count)
        clipped = jnp.clip(micro_index, 0, micro_count - 1)
        from_heads = lax.dynamic_index_in_dim(cotangents, clipped, 0, keepdims=False)
        current = jnp.where(my_section == sections - 1, from_heads, incoming)
        inputs = lax.dynamic_index_in_dim(saved, clipped, 0, keepdims=False)
        active, inner, passed = section_back(inputs, down_map, up_map, current)
        grad_rows = store_row(grad_rows, current, clipped, valid)
        active_rows = store_row(active_rows, active, clipped, valid)
        inner_rows = store_row(inner_rows, inner, clipped, valid)
        incoming = from_behind(passed, "section", -1)
        return (incoming, grad_rows, active_rows, inner_rows)

    start_carry = (
        jnp.zeros((tok_rows, dim_model), jnp.bfloat16),
        jnp.zeros((micro_count, tok_rows, dim_model), jnp.bfloat16),
        jnp.zeros((micro_count, tok_rows, rank_width), jnp.bfloat16),
        jnp.zeros((micro_count, tok_rows, rank_width), jnp.bfloat16),
    )
    finished = lax.fori_loop(0, micro_count + sections - 1, tick, start_carry)
    grad_rows = finished[1]
    active_rows = finished[2]
    inner_rows = finished[3]
    part_down = jnp.einsum("mtd,mtr->dr", saved, inner_rows, preferred_element_type=jnp.float32)
    part_up = jnp.einsum("mtd,mtr->dr", grad_rows, active_rows, preferred_element_type=jnp.float32)
    shares = lax.psum_scatter(
        jnp.concatenate([part_down, part_up], axis=1).astype(jnp.bfloat16),
        "dp",
        scatter_dimension=0,
        tiled=True,
    ).astype(jnp.float32)
    grad_down = shares[:, :rank_width]
    grad_up = shares[:, rank_width:]
    return (grad_down[None], grad_up[None], mixing)


def solution(mesh):
    in_specs = (
        P("section", None, "dp", None),
        P("section", None, None),
        P("section", None, None),
        P("section", "dp", None),
        P("dp", None),
        P("section", "dp", None),
        P(),
    )
    out_specs = (P("section", "dp", None), P("section", "dp", None), P())
    return jax.shard_map(body, mesh=mesh, in_specs=in_specs, out_specs=out_specs, check_vma=False)
```

profile of v0, /device:TPU:4, one launch (start us, length us, event | category | flops | bytes accessed | tf_op | source)
XLA Modules:
  0.0 765.6 jit_solution(4357182135453760184)
XLA Ops:
  8.8 82.9 %all-gather.4.cloned.1.call-done = bf16[8192,128]{1,0:T(8,128)(2,1)} async-done(((bf16[256,128]{1,0:T(8,128)(2,1)}), bf16[8192,128]{1,0:T(8,128)(2,1)}) %all-gather.4.cloned.1.call-update) | async-done | bytes 2097168 | tf_op jit(solution)/shard_map/all_gather | solution.py:65
  96.3 24.6 %fusion.22 = f32[6,6]{1,0:T(8,128)S(1)} fusion(f32[6,32,8192]{2,1,0:T(8,128)S(1)} %fusion.19), kind=kOutput, calls=%fused_computation.43 | convolution fusion | flops 113246208 | bytes 6291600 | tf_op jit(solution)/shard_map/atd,btd->ab/dot_general | solution.py:74
  120.9 72.7 %psum.7 = f32[6,6]{1,0:T(8,128)S(1)} all-reduce(f32[6,6]{1,0:T(8,128)S(1)} %fusion.22), channel_id=1, replica_groups=mesh['section'=8,'dp'=32] {'section','dp'}, use_global_device_ids=true, to_apply=%region_0.0 | all-reduce | flops 36 | bytes 288 | tf_op jit(solution)/shard_map/psum | solution.py:77
  194.8 28.4 %while.33 = (s32[]{:T(128)}, f32[6]{0:T(128)S(1)}, f32[6,6]{1,0:T(8,128)S(1)}, f32[]{:T(128)}, s32[]{:T(128)}, /*index=5*/s32[]{:T(128)}) while((s32[]{:T(128)}, f32[6]{0:T(128)S(1)}, f32[6,6]{1,0:T(8,128)S(1)}, f32[]{:T(128)}, s32[]{:T(128)}, /*index=5*/s32[]{:T(128)}) %tuple.73), condition=%wide.region_4.5_spmd.clone, body=%wide.region_2.4_spmd.clone.sunk | while | flops 476 | bytes 331 | solution.py:50
  226.9 29.7 %all-gather.6.cloned.1.call-done = bf16[256,8192]{1,0:T(8,128)(2,1)} async-done(((bf16[32,8192]{1,0:T(8,128)(2,1)}), bf16[256,8192]{1,0:T(8,128)(2,1)}) %all-gather.6.cloned.1.call-update) | async-done | bytes 4194320 | tf_op jit(solution)/shard_map/all_gather | solution.py:84
  259.2 263.7 %while.32 = (s32[]{:T(128)}, bf16[32,8192]{1,0:T(8,128)(2,1)S(1)}, bf16[8,32,8192]{2,1,0:T(8,128)(2,1)}, bf16[8,32,128]{2,1,0:T(8,128)(2,1)S(1)}, bf16[8,32,128]...) while((s32[]{:T(128)}, bf16[32,8192]{1,0:T(8,128)(2,1)S(1)}, ...), condition=%wide.region_6.7_spmd, body=%wide.region_5.6_spmd.sunk | while | flops 202702848 | bytes 22661404 | solution.py:107
  268.7 7.0 collective-permute-done
  286.3 7.0 collective-permute-done
  304.0 7.0 collective-permute-done
  321.6 7.0 collective-permute-done
  339.3 7.0 collective-permute-done
  356.9 7.0 collective-permute-done
  370.8 3.7 collective-permute-start
  374.6 7.0 collective-permute-done
  392.2 7.0 collective-permute-done
  406.1 3.7 collective-permute-start
  409.8 7.0 collective-permute-done
  427.5 7.0 collective-permute-done
  445.1 7.0 collective-permute-done
  462.8 7.0 collective-permute-done
  480.5 7.0 collective-permute-done
  498.2 7.0 collective-permute-done
  515.9 7.0 collective-permute-done
  529.5 227.1 %reduce-scatter.2.cloned.1.call-done = bf16[256,256]{0,1:T(8,128)(2,1)} async-done(((bf16[8192,256]{0,1:T(8,128)(2,1)}), bf16[256,256]{0,1:T(8,128)(2,1)}) %reduce-scatter.2.cloned.1.call-update) | async-done | bytes 131088 | tf_op jit(solution)/shard_map/reduce_scatter | solution.py:113
  (207 shorter events, 200.8 us)
Async XLA Ops:
  7.2 84.5 %copy-start = (bf16[1,32,8192]{2,1,0:T(8,128)(2,1)S(1)}, bf16[1,32,8192]{2,1,0:T(8,128)(2,1)}, u32[]{:S(2)}) copy-start(bf16[1,32,8192]{2,1,0:T(8,128)(2,1)} %param.14) | copy-start | bytes 1572868
  7.2 84.5 %all-gather.4.cloned.1.call-start = ((), (), s32[]{:S(2)}) async-start(), calls=%async_computation.1 | async-start | bytes 2162688 | tf_op jit(solution)/shard_map/all_gather | solution.py:65
  7.9 248.7 %all-gather.6.cloned.1.call-start = ((), (), s32[]{:S(2)}) async-start(), calls=%async_computation.3 | async-start | bytes 4718592 | tf_op jit(solution)/shard_map/all_gather | solution.py:84
  120.9 138.3 %copy-start.1 = (bf16[1,8192,128]{2,1,0:T(8,128)(2,1)S(1)}, bf16[1,8192,128]{2,1,0:T(8,128)(2,1)}, u32[]{:S(2)}) copy-start(bf16[1,8192,128]{2,1,0:T(8,128)(2,1)} %param.12) | copy-start | bytes 6291460
  223.2 35.9 %copy-start.4 = (f32[6]{0:T(128)}, f32[6]{0:T(128)S(1)}, u32[]{:S(2)}) copy-start(f32[6]{0:T(128)S(1)} %get-tuple-element.286) | copy-start | bytes 76
  226.6 530.0 %reduce-scatter.2.cloned.1.call-start = ((), (), s32[]{:S(2)}) async-start(), calls=%async_computation.2 | async-start | bytes 4325376 | tf_op jit(solution)/shard_map/reduce_scatter | solution.py:113
  266.1 9.6 %collective-permute-start = (bf16[32,8192]{1,0:T(8,128)(2,1)}, bf16[32,8192]{1,0:T(8,128)(2,1)S(1)}, u32[]{:S(2)}, u32[]{:S(2)}) collective-permute-start(bf16[32,8192]{1,0:T(8,128)(2,1)} %fusion.58), channel_id=1, source_target_pairs={{32,0},{64,32},{96,64},{128,96},{160,128},{192,160},{224,192},{33,... | collective-permute-start | bytes 1572872 | tf_op jit(solution)/shard_map/while/body/eval_jaxpr/ppermute | solution.py:15
  282.6 10.7 %collective-permute-start = (bf16[32,8192]{1,0:T(8,128)(2,1)}, bf16[32,8192]{1,0:T(8,128)(2,1)S(1)}, u32[]{:S(2)}, u32[]{:S(2)}) collective-permute-start(bf16[32,8192]{1,0:T(8,128)(2,1)} %fusion.58), channel_id=1, source_target_pairs={{32,0},{64,32},{96,64},{128,96},{160,128},{192,160},{224,192},{33,... | collective-permute-start | bytes 1572872 | tf_op jit(solution)/shard_map/while/body/eval_jaxpr/ppermute | solution.py:15
  300.3 10.7 %collective-permute-start = (bf16[32,8192]{1,0:T(8,128)(2,1)}, bf16[32,8192]{1,0:T(8,128)(2,1)S(1)}, u32[]{:S(2)}, u32[]{:S(2)}) collective-permute-start(bf16[32,8192]{1,0:T(8,128)(2,1)} %fusion.58), channel_id=1, source_target_pairs={{32,0},{64,32},{96,64},{128,96},{160,128},{192,160},{224,192},{33,... | collective-permute-start | bytes 1572872 | tf_op jit(solution)/shard_map/while/body/eval_jaxpr/ppermute | solution.py:15
  317.9 10.7 %collective-permute-start = (bf16[32,8192]{1,0:T(8,128)(2,1)}, bf16[32,8192]{1,0:T(8,128)(2,1)S(1)}, u32[]{:S(2)}, u32[]{:S(2)}) collective-permute-start(bf16[32,8192]{1,0:T(8,128)(2,1)} %fusion.58), channel_id=1, source_target_pairs={{32,0},{64,32},{96,64},{128,96},{160,128},{192,160},{224,192},{33,... | collective-permute-start | bytes 1572872 | tf_op jit(solution)/shard_map/while/body/eval_jaxpr/ppermute | solution.py:15
  335.5 10.7 %collective-permute-start = (bf16[32,8192]{1,0:T(8,128)(2,1)}, bf16[32,8192]{1,0:T(8,128)(2,1)S(1)}, u32[]{:S(2)}, u32[]{:S(2)}) collective-permute-start(bf16[32,8192]{1,0:T(8,128)(2,1)} %fusion.58), channel_id=1, source_target_pairs={{32,0},{64,32},{96,64},{128,96},{160,128},{192,160},{224,192},{33,... | collective-permute-start | bytes 1572872 | tf_op jit(solution)/shard_map/while/body/eval_jaxpr/ppermute | solution.py:15
  353.2 10.7 %collective-permute-start = (bf16[32,8192]{1,0:T(8,128)(2,1)}, bf16[32,8192]{1,0:T(8,128)(2,1)S(1)}, u32[]{:S(2)}, u32[]{:S(2)}) collective-permute-start(bf16[32,8192]{1,0:T(8,128)(2,1)} %fusion.58), channel_id=1, source_target_pairs={{32,0},{64,32},{96,64},{128,96},{160,128},{192,160},{224,192},{33,... | collective-permute-start | bytes 1572872 | tf_op jit(solution)/shard_map/while/body/eval_jaxpr/ppermute | solution.py:15
  370.8 10.7 %collective-permute-start = (bf16[32,8192]{1,0:T(8,128)(2,1)}, bf16[32,8192]{1,0:T(8,128)(2,1)S(1)}, u32[]{:S(2)}, u32[]{:S(2)}) collective-permute-start(bf16[32,8192]{1,0:T(8,128)(2,1)} %fusion.58), channel_id=1, source_target_pairs={{32,0},{64,32},{96,64},{128,96},{160,128},{192,160},{224,192},{33,... | collective-permute-start | bytes 1572872 | tf_op jit(solution)/shard_map/while/body/eval_jaxpr/ppermute | solution.py:15
  388.5 10.7 %collective-permute-start = (bf16[32,8192]{1,0:T(8,128)(2,1)}, bf16[32,8192]{1,0:T(8,128)(2,1)S(1)}, u32[]{:S(2)}, u32[]{:S(2)}) collective-permute-start(bf16[32,8192]{1,0:T(8,128)(2,1)} %fusion.58), channel_id=1, source_target_pairs={{32,0},{64,32},{96,64},{128,96},{160,128},{192,160},{224,192},{33,... | collective-permute-start | bytes 1572872 | tf_op jit(solution)/shard_map/while/body/eval_jaxpr/ppermute | solution.py:15
  406.1 10.7 %collective-permute-start = (bf16[32,8192]{1,0:T(8,128)(2,1)}, bf16[32,8192]{1,0:T(8,128)(2,1)S(1)}, u32[]{:S(2)}, u32[]{:S(2)}) collective-permute-start(bf16[32,8192]{1,0:T(8,128)(2,1)} %fusion.58), channel_id=1, source_target_pairs={{32,0},{64,32},{96,64},{128,96},{160,128},{192,160},{224,192},{33,... | collective-permute-start | bytes 1572872 | tf_op jit(solution)/shard_map/while/body/eval_jaxpr/ppermute | solution.py:15
  423.8 10.7 %collective-permute-start = (bf16[32,8192]{1,0:T(8,128)(2,1)}, bf16[32,8192]{1,0:T(8,128)(2,1)S(1)}, u32[]{:S(2)}, u32[]{:S(2)}) collective-permute-start(bf16[32,8192]{1,0:T(8,128)(2,1)} %fusion.58), channel_id=1, source_target_pairs={{32,0},{64,32},{96,64},{128,96},{160,128},{192,160},{224,192},{33,... | collective-permute-start | bytes 1572872 | tf_op jit(solution)/shard_map/while/body/eval_jaxpr/ppermute | solution.py:15
  434.5 4.9 copy-start.2
  441.5 10.6 %collective-permute-start = (bf16[32,8192]{1,0:T(8,128)(2,1)}, bf16[32,8192]{1,0:T(8,128)(2,1)S(1)}, u32[]{:S(2)}, u32[]{:S(2)}) collective-permute-start(bf16[32,8192]{1,0:T(8,128)(2,1)} %fusion.58), channel_id=1, source_target_pairs={{32,0},{64,32},{96,64},{128,96},{160,128},{192,160},{224,192},{33,... | collective-permute-start | bytes 1572872 | tf_op jit(solution)/shard_map/while/body/eval_jaxpr/ppermute | solution.py:15
  452.1 4.9 copy-start.2
  459.1 10.7 %collective-permute-start = (bf16[32,8192]{1,0:T(8,128)(2,1)}, bf16[32,8192]{1,0:T(8,128)(2,1)S(1)}, u32[]{:S(2)}, u32[]{:S(2)}) collective-permute-start(bf16[32,8192]{1,0:T(8,128)(2,1)} %fusion.58), channel_id=1, source_target_pairs={{32,0},{64,32},{96,64},{128,96},{160,128},{192,160},{224,192},{33,... | collective-permute-start | bytes 1572872 | tf_op jit(solution)/shard_map/while/body/eval_jaxpr/ppermute | solution.py:15
  476.8 10.7 %collective-permute-start = (bf16[32,8192]{1,0:T(8,128)(2,1)}, bf16[32,8192]{1,0:T(8,128)(2,1)S(1)}, u32[]{:S(2)}, u32[]{:S(2)}) collective-permute-start(bf16[32,8192]{1,0:T(8,128)(2,1)} %fusion.58), channel_id=1, source_target_pairs={{32,0},{64,32},{96,64},{128,96},{160,128},{192,160},{224,192},{33,... | collective-permute-start | bytes 1572872 | tf_op jit(solution)/shard_map/while/body/eval_jaxpr/ppermute | solution.py:15
  487.5 4.9 copy-start.2
  494.5 10.7 %collective-permute-start = (bf16[32,8192]{1,0:T(8,128)(2,1)}, bf16[32,8192]{1,0:T(8,128)(2,1)S(1)}, u32[]{:S(2)}, u32[]{:S(2)}) collective-permute-start(bf16[32,8192]{1,0:T(8,128)(2,1)} %fusion.58), channel_id=1, source_target_pairs={{32,0},{64,32},{96,64},{128,96},{160,128},{192,160},{224,192},{33,... | collective-permute-start | bytes 1572872 | tf_op jit(solution)/shard_map/while/body/eval_jaxpr/ppermute | solution.py:15
  512.2 10.7 %collective-permute-start = (bf16[32,8192]{1,0:T(8,128)(2,1)}, bf16[32,8192]{1,0:T(8,128)(2,1)S(1)}, u32[]{:S(2)}, u32[]{:S(2)}) collective-permute-start(bf16[32,8192]{1,0:T(8,128)(2,1)} %fusion.58), channel_id=1, source_target_pairs={{32,0},{64,32},{96,64},{128,96},{160,128},{192,160},{224,192},{33,... | collective-permute-start | bytes 1572872 | tf_op jit(solution)/shard_map/while/body/eval_jaxpr/ppermute | solution.py:15
  (13 other events, 61.5 us)
Sparse Core Ops, SparseCore 0:
  10.6 81.0 all-gather.3
  226.7 29.8 all-gather.5
  529.6 226.9 reduce-scatter.1
where the time goes:
time: 768 us; the launch traced here: 766 us
  waiting for transfers between devices  445 us (58%)
  matrix products  106 us (14%)
  blocking collectives  72.7 us (9%)
  starting transfers between devices  54.6 us (7%)
  other arithmetic  48 us (6%)
  local copies, waits for them, and re-layouts  23.8 us (3%)
  between operations  14.5 us (2%)
    reduce_scatter x1, waiting for transfers between devices, body(): lax.psum_scatter(jnp.concatenate([part_down, part_up], axis=1).astype(jnp...  227 us
    ppermute x15, waiting for transfers between devices, from_behind(): lax.ppermute(value, axis, [(source, source + steps) for source in range(f...  105 us
    all_gather x1, waiting for transfers between devices, body(): weights = lax.all_gather(head_weights, 'dp', axis=0, tiled=True)  82.9 us
    psum x1, blocking collectives, body(): gram_matrix = lax.psum(partial_gram, ('section', 'dp'))  72.7 us
    ppermute x15, starting transfers between devices, from_behind(): lax.ppermute(value, axis, [(source, source + steps) for source in range(f...  54.3 us
    dynamic_update_slice x15, other arithmetic, store_row(): return lax.dynamic_update_index_in_dim(buffer, chosen, index, 0)  31.1 us
    all_gather x1, waiting for transfers between devices, body(): cotangents = lax.all_gather(own_grad[None], 'section', axis=0, tiled=True)  29.7 us
    dot_general x15, matrix products, section_back(): lax.dot_general(inner, down_map, (((1,), (1,)), ((), ())), preferred_elem...  24.8 us
  transfers between devices with their start and end apart: 18, of which 18 were waited for; matrix products, arithmetic and copies ran while one was open for 0% of the time, Pallas kernels for 0%

commit v1 on v0

--- a/solution.py
+++ b/solution.py
@@ -81,7 +81,10 @@
     own_grad = jnp.einsum(
         "tc,dc->td", weighted, weights, preferred_element_type=jnp.float32
     ).astype(jnp.bfloat16)
-    cotangents = lax.all_gather(own_grad[None], "section", axis=0, tiled=True)
+    cotangents = jnp.concatenate(
+        lax.all_to_all(jnp.stack([own_grad[None]] * lax.axis_size("section")), "section", 0, 0),
+        axis=0,
+    )
 
     def tick(counter, carry):
         incoming, grad_rows, active_rows, inner_rows = carry

time: 768 us -> 788 us (1.026)
  waiting for transfers between devices: 445 us -> 458 us
    all_to_all x0 -> x1, waiting for transfers between devices: none -> 46.6 us  [body(): lax.all_to_all(jnp.stack([own_grad[None]] * lax.axis_size('section')), 's...]
    all_gather x1 -> x0, waiting for transfers between devices: 29.7 us -> none  [body(): cotangents = lax.all_gather(own_grad[None], 'section', axis=0, tiled=True)]
where the time goes in v1:
time: 788 us; the launch traced here: 785 us
  waiting for transfers between devices  458 us (58%)
  matrix products  103 us (13%)
  blocking collectives  72.7 us (9%)
  starting transfers between devices  61.8 us (8%)
  other arithmetic  48 us (6%)
  local copies, waits for them, and re-layouts  26.3 us (3%)
  between operations  14.8 us (2%)
    reduce_scatter x1, waiting for transfers between devices, body(): lax.psum_scatter(jnp.concatenate([part_down, part_up], axis=1).astype(jnp...  222 us
    ppermute x15, waiting for transfers between devices, from_behind(): lax.ppermute(value, axis, [(source, source + steps) for source in range(f...  105 us
    all_gather x1, waiting for transfers between devices, body(): weights = lax.all_gather(head_weights, 'dp', axis=0, tiled=True)  82.9 us
    psum x1, blocking collectives, body(): gram_matrix = lax.psum(partial_gram, ('section', 'dp'))  72.7 us
    ppermute x15, starting transfers between devices, from_behind(): lax.ppermute(value, axis, [(source, source + steps) for source in range(f...  55 us
    all_to_all x1, waiting for transfers between devices, body(): lax.all_to_all(jnp.stack([own_grad[None]] * lax.axis_size('section')), 's...  46.6 us
    dynamic_update_slice x15, other arithmetic, store_row(): return lax.dynamic_update_index_in_dim(buffer, chosen, index, 0)  31.1 us
    dot_general x15, matrix products, section_back(): lax.dot_general(inner, down_map, (((1,), (1,)), ((), ())), preferred_elem...  24.8 us
  transfers between devices with their start and end apart: 18, of which 18 were waited for; matrix products, arithmetic and copies ran while one was open for 0% of the time, Pallas kernels for 0%

profile of v1, /device:TPU:4, one launch (start us, length us, event | category | flops | bytes accessed | tf_op | source)
XLA Modules:
  0.0 785.4 jit_solution(10046241042696576582)
XLA Ops:
  8.7 82.9 %all-gather.2.cloned.1.call-done = bf16[8192,128]{1,0:T(8,128)(2,1)} async-done(((bf16[256,128]{1,0:T(8,128)(2,1)}), bf16[8192,128]{1,0:T(8,128)(2,1)}) %all-gather.2.cloned.1.call-update) | async-done | bytes 2097168 | tf_op jit(solution)/shard_map/all_gather | solution.py:65
  96.3 24.6 %fusion.22 = f32[6,6]{1,0:T(8,128)S(1)} fusion(f32[6,32,8192]{2,1,0:T(8,128)S(1)} %fusion.19), kind=kOutput, calls=%fused_computation.43 | convolution fusion | flops 113246208 | bytes 6291600 | tf_op jit(solution)/shard_map/atd,btd->ab/dot_general | solution.py:74
  120.9 72.7 %psum.7 = f32[6,6]{1,0:T(8,128)S(1)} all-reduce(f32[6,6]{1,0:T(8,128)S(1)} %fusion.22), channel_id=1, replica_groups=mesh['section'=8,'dp'=32] {'section','dp'}, use_global_device_ids=true, to_apply=%region_0.0 | all-reduce | flops 36 | bytes 288 | tf_op jit(solution)/shard_map/psum | solution.py:77
  194.8 28.4 %while.33 = (s32[]{:T(128)}, f32[6]{0:T(128)S(1)}, f32[6,6]{1,0:T(8,128)S(1)}, f32[]{:T(128)}, s32[]{:T(128)}, /*index=5*/s32[]{:T(128)}) while((s32[]{:T(128)}, f32[6]{0:T(128)S(1)}, f32[6,6]{1,0:T(8,128)S(1)}, f32[]{:T(128)}, s32[]{:T(128)}, /*index=5*/s32[]{:T(128)}) %tuple.74), condition=%wide.region_4.5_spmd.clone, body=%wide.region_2.4_spmd.clone.sunk | while | flops 476 | bytes 331 | solution.py:50
  226.7 6.8 all-to-all-start
  233.5 46.6 %all-to-all-done = bf16[8,1,32,8192]{3,2,1,0:T(8,128)(2,1)} async-done(((bf16[8,1,32,8192]{3,2,1,0:T(8,128)(2,1)}), bf16[8,1,32,8192]{3,2,1,0:T(8,128)(2,1)}, u32[]{:S(2)}, u32[]{:S(2)}) %all-to-all-start) | async-done | bytes 4194336 | tf_op jit(solution)/shard_map/all_to_all | solution.py:85
  282.6 264.4 %while.32 = (s32[]{:T(128)}, bf16[32,8192]{1,0:T(8,128)(2,1)S(1)}, bf16[8,32,8192]{2,1,0:T(8,128)(2,1)}, bf16[8,32,128]{2,1,0:T(8,128)(2,1)S(1)}, bf16[8,32,128]...) while((s32[]{:T(128)}, bf16[32,8192]{1,0:T(8,128)(2,1)S(1)}, ...), condition=%wide.region_6.7_spmd, body=%wide.region_5.6_spmd.sunk | while | flops 202702848 | bytes 22661404 | solution.py:110
  292.8 7.0 collective-permute-done
  310.5 7.0 collective-permute-done
  328.1 7.0 collective-permute-done
  345.7 7.0 collective-permute-done
  363.4 7.0 collective-permute-done
  381.0 7.0 collective-permute-done
  394.9 3.7 collective-permute-start
  398.7 7.0 collective-permute-done
  416.3 7.0 collective-permute-done
  433.9 7.0 collective-permute-done
  451.6 7.0 collective-permute-done
  469.2 7.0 collective-permute-done
  486.9 7.0 collective-permute-done
  504.6 7.0 collective-permute-done
  522.3 7.0 collective-permute-done
  540.0 7.0 collective-permute-done
  553.6 222.5 %reduce-scatter.2.cloned.1.call-done = bf16[256,256]{0,1:T(8,128)(2,1)} async-done(((bf16[8192,256]{0,1:T(8,128)(2,1)}), bf16[256,256]{0,1:T(8,128)(2,1)}) %reduce-scatter.2.cloned.1.call-update) | async-done | bytes 131088 | tf_op jit(solution)/shard_map/reduce_scatter | solution.py:116
  (209 shorter events, 205.0 us)
Async XLA Ops:
  7.2 84.5 %copy-start = (bf16[1,32,8192]{2,1,0:T(8,128)(2,1)S(1)}, bf16[1,32,8192]{2,1,0:T(8,128)(2,1)}, u32[]{:S(2)}) copy-start(bf16[1,32,8192]{2,1,0:T(8,128)(2,1)} %param.14) | copy-start | bytes 1572868
  7.2 84.5 %all-gather.2.cloned.1.call-start = ((), (), s32[]{:S(2)}) async-start(), calls=%async_computation.2 | async-start | bytes 2162688 | tf_op jit(solution)/shard_map/all_gather | solution.py:65
  96.3 127.1 %copy-start.4 = (bf16[8192,128]{1,0:T(8,128)(2,1)S(1)}, bf16[8192,128]{1,0:T(8,128)(2,1)}, u32[]{:S(2)}) copy-start(bf16[8192,128]{1,0:T(8,128)(2,1)} %all-gather.2.cloned.1.call-done) | copy-start | bytes 6291460
  226.7 53.3 %all-to-all-start = ((bf16[8,1,32,8192]{3,2,1,0:T(8,128)(2,1)}), bf16[8,1,32,8192]{3,2,1,0:T(8,128)(2,1)}, u32[]{:S(2)}, u32[]{:S(2)}) async-start(bf16[8,1,32,8192]{3,2,1,0:T(8,128)(2,1)} %stack.3), calls=%async_computation | async-start | bytes 8388608 | tf_op jit(solution)/shard_map/all_to_all | solution.py:85
  233.4 49.1 %copy-start.1 = (bf16[1,8192,128]{2,1,0:T(8,128)(2,1)S(1)}, bf16[1,8192,128]{2,1,0:T(8,128)(2,1)}, u32[]{:S(2)}) copy-start(bf16[1,8192,128]{2,1,0:T(8,128)(2,1)} %param.12) | copy-start | bytes 6291460
  233.4 542.7 %reduce-scatter.2.cloned.1.call-start = ((), (), s32[]{:S(2)}) async-start(), calls=%async_computation.3 | async-start | bytes 4325376 | tf_op jit(solution)/shard_map/reduce_scatter | solution.py:116
  289.5 10.3 %collective-permute-start = (bf16[32,8192]{1,0:T(8,128)(2,1)}, bf16[32,8192]{1,0:T(8,128)(2,1)S(1)}, u32[]{:S(2)}, u32[]{:S(2)}) collective-permute-start(bf16[32,8192]{1,0:T(8,128)(2,1)} %fusion.58), channel_id=1, source_target_pairs={{32,0},{64,32},{96,64},{128,96},{160,128},{192,160},{224,192},{33,... | collective-permute-start | bytes 1572872 | tf_op jit(solution)/shard_map/while/body/eval_jaxpr/ppermute | solution.py:15
  306.8 10.7 %collective-permute-start = (bf16[32,8192]{1,0:T(8,128)(2,1)}, bf16[32,8192]{1,0:T(8,128)(2,1)S(1)}, u32[]{:S(2)}, u32[]{:S(2)}) collective-permute-start(bf16[32,8192]{1,0:T(8,128)(2,1)} %fusion.58), channel_id=1, source_target_pairs={{32,0},{64,32},{96,64},{128,96},{160,128},{192,160},{224,192},{33,... | collective-permute-start | bytes 1572872 | tf_op jit(solution)/shard_map/while/body/eval_jaxpr/ppermute | solution.py:15
  324.4 10.7 %collective-permute-start = (bf16[32,8192]{1,0:T(8,128)(2,1)}, bf16[32,8192]{1,0:T(8,128)(2,1)S(1)}, u32[]{:S(2)}, u32[]{:S(2)}) collective-permute-start(bf16[32,8192]{1,0:T(8,128)(2,1)} %fusion.58), channel_id=1, source_target_pairs={{32,0},{64,32},{96,64},{128,96},{160,128},{192,160},{224,192},{33,... | collective-permute-start | bytes 1572872 | tf_op jit(solution)/shard_map/while/body/eval_jaxpr/ppermute | solution.py:15
  342.0 10.7 %collective-permute-start = (bf16[32,8192]{1,0:T(8,128)(2,1)}, bf16[32,8192]{1,0:T(8,128)(2,1)S(1)}, u32[]{:S(2)}, u32[]{:S(2)}) collective-permute-start(bf16[32,8192]{1,0:T(8,128)(2,1)} %fusion.58), channel_id=1, source_target_pairs={{32,0},{64,32},{96,64},{128,96},{160,128},{192,160},{224,192},{33,... | collective-permute-start | bytes 1572872 | tf_op jit(solution)/shard_map/while/body/eval_jaxpr/ppermute | solution.py:15
  359.7 10.7 %collective-permute-start = (bf16[32,8192]{1,0:T(8,128)(2,1)}, bf16[32,8192]{1,0:T(8,128)(2,1)S(1)}, u32[]{:S(2)}, u32[]{:S(2)}) collective-permute-start(bf16[32,8192]{1,0:T(8,128)(2,1)} %fusion.58), channel_id=1, source_target_pairs={{32,0},{64,32},{96,64},{128,96},{160,128},{192,160},{224,192},{33,... | collective-permute-start | bytes 1572872 | tf_op jit(solution)/shard_map/while/body/eval_jaxpr/ppermute | solution.py:15
  377.3 10.7 %collective-permute-start = (bf16[32,8192]{1,0:T(8,128)(2,1)}, bf16[32,8192]{1,0:T(8,128)(2,1)S(1)}, u32[]{:S(2)}, u32[]{:S(2)}) collective-permute-start(bf16[32,8192]{1,0:T(8,128)(2,1)} %fusion.58), channel_id=1, source_target_pairs={{32,0},{64,32},{96,64},{128,96},{160,128},{192,160},{224,192},{33,... | collective-permute-start | bytes 1572872 | tf_op jit(solution)/shard_map/while/body/eval_jaxpr/ppermute | solution.py:15
  394.9 10.7 %collective-permute-start = (bf16[32,8192]{1,0:T(8,128)(2,1)}, bf16[32,8192]{1,0:T(8,128)(2,1)S(1)}, u32[]{:S(2)}, u32[]{:S(2)}) collective-permute-start(bf16[32,8192]{1,0:T(8,128)(2,1)} %fusion.58), channel_id=1, source_target_pairs={{32,0},{64,32},{96,64},{128,96},{160,128},{192,160},{224,192},{33,... | collective-permute-start | bytes 1572872 | tf_op jit(solution)/shard_map/while/body/eval_jaxpr/ppermute | solution.py:15
  412.6 10.7 %collective-permute-start = (bf16[32,8192]{1,0:T(8,128)(2,1)}, bf16[32,8192]{1,0:T(8,128)(2,1)S(1)}, u32[]{:S(2)}, u32[]{:S(2)}) collective-permute-start(bf16[32,8192]{1,0:T(8,128)(2,1)} %fusion.58), channel_id=1, source_target_pairs={{32,0},{64,32},{96,64},{128,96},{160,128},{192,160},{224,192},{33,... | collective-permute-start | bytes 1572872 | tf_op jit(solution)/shard_map/while/body/eval_jaxpr/ppermute | solution.py:15
  430.2 10.7 %collective-permute-start = (bf16[32,8192]{1,0:T(8,128)(2,1)}, bf16[32,8192]{1,0:T(8,128)(2,1)S(1)}, u32[]{:S(2)}, u32[]{:S(2)}) collective-permute-start(bf16[32,8192]{1,0:T(8,128)(2,1)} %fusion.58), channel_id=1, source_target_pairs={{32,0},{64,32},{96,64},{128,96},{160,128},{192,160},{224,192},{33,... | collective-permute-start | bytes 1572872 | tf_op jit(solution)/shard_map/while/body/eval_jaxpr/ppermute | solution.py:15
  447.9 10.7 %collective-permute-start = (bf16[32,8192]{1,0:T(8,128)(2,1)}, bf16[32,8192]{1,0:T(8,128)(2,1)S(1)}, u32[]{:S(2)}, u32[]{:S(2)}) collective-permute-start(bf16[32,8192]{1,0:T(8,128)(2,1)} %fusion.58), channel_id=1, source_target_pairs={{32,0},{64,32},{96,64},{128,96},{160,128},{192,160},{224,192},{33,... | collective-permute-start | bytes 1572872 | tf_op jit(solution)/shard_map/while/body/eval_jaxpr/ppermute | solution.py:15
  458.6 4.9 copy-start.2
  465.6 10.6 %collective-permute-start = (bf16[32,8192]{1,0:T(8,128)(2,1)}, bf16[32,8192]{1,0:T(8,128)(2,1)S(1)}, u32[]{:S(2)}, u32[]{:S(2)}) collective-permute-start(bf16[32,8192]{1,0:T(8,128)(2,1)} %fusion.58), channel_id=1, source_target_pairs={{32,0},{64,32},{96,64},{128,96},{160,128},{192,160},{224,192},{33,... | collective-permute-start | bytes 1572872 | tf_op jit(solution)/shard_map/while/body/eval_jaxpr/ppermute | solution.py:15
  476.2 4.9 copy-start.2
  483.2 10.7 %collective-permute-start = (bf16[32,8192]{1,0:T(8,128)(2,1)}, bf16[32,8192]{1,0:T(8,128)(2,1)S(1)}, u32[]{:S(2)}, u32[]{:S(2)}) collective-permute-start(bf16[32,8192]{1,0:T(8,128)(2,1)} %fusion.58), channel_id=1, source_target_pairs={{32,0},{64,32},{96,64},{128,96},{160,128},{192,160},{224,192},{33,... | collective-permute-start | bytes 1572872 | tf_op jit(solution)/shard_map/while/body/eval_jaxpr/ppermute | solution.py:15
  500.9 10.7 %collective-permute-start = (bf16[32,8192]{1,0:T(8,128)(2,1)}, bf16[32,8192]{1,0:T(8,128)(2,1)S(1)}, u32[]{:S(2)}, u32[]{:S(2)}) collective-permute-start(bf16[32,8192]{1,0:T(8,128)(2,1)} %fusion.58), channel_id=1, source_target_pairs={{32,0},{64,32},{96,64},{128,96},{160,128},{192,160},{224,192},{33,... | collective-permute-start | bytes 1572872 | tf_op jit(solution)/shard_map/while/body/eval_jaxpr/ppermute | solution.py:15
  511.6 4.9 copy-start.2
  518.6 10.7 %collective-permute-start = (bf16[32,8192]{1,0:T(8,128)(2,1)}, bf16[32,8192]{1,0:T(8,128)(2,1)S(1)}, u32[]{:S(2)}, u32[]{:S(2)}) collective-permute-start(bf16[32,8192]{1,0:T(8,128)(2,1)} %fusion.58), channel_id=1, source_target_pairs={{32,0},{64,32},{96,64},{128,96},{160,128},{192,160},{224,192},{33,... | collective-permute-start | bytes 1572872 | tf_op jit(solution)/shard_map/while/body/eval_jaxpr/ppermute | solution.py:15
  536.3 10.7 %collective-permute-start = (bf16[32,8192]{1,0:T(8,128)(2,1)}, bf16[32,8192]{1,0:T(8,128)(2,1)S(1)}, u32[]{:S(2)}, u32[]{:S(2)}) collective-permute-start(bf16[32,8192]{1,0:T(8,128)(2,1)} %fusion.58), channel_id=1, source_target_pairs={{32,0},{64,32},{96,64},{128,96},{160,128},{192,160},{224,192},{33,... | collective-permute-start | bytes 1572872 | tf_op jit(solution)/shard_map/while/body/eval_jaxpr/ppermute | solution.py:15
  (14 other events, 64.9 us)
Sparse Core Ops, SparseCore 0:
  10.6 81.0 all-gather.1
  553.7 222.3 reduce-scatter.1
